TPU v7x, 512 devices: a whole 4x8x8 slice. The times are simulated.
512 devices in a mesh: dp: 32 (over x_lo, y, core), tensor: 16 (over x_hi, z).
Axes of the slice: x: 4 (x_hi: 2, x_lo: 2; x = x_hi * 2 + x_lo), y: 8, z: 8, core: 2. Of those that a mesh axis runs over, the one named last changes fastest.
Arguments:
- tokens: bfloat16 [8192, 4096], P(('dp', 'tensor')), may hold values from -110 to 110
- norm_gain: bfloat16 [4096], replicated, may hold values from 0.099609375 to 1.8984375
- query_weight: bfloat16 [4096, 4096], P('dp', 'tensor'), may hold values from -1 to 1
- kv_weight: bfloat16 [4096, 1024], P('dp', 'tensor'), may hold values from -1 to 1
- out_weight: bfloat16 [4096, 4096], P('tensor', 'dp'), may hold values from -0.09375 to 0.09375
- grad_out: bfloat16 [8192, 4096], P(('dp', 'tensor')), may hold values from -6 to 6
- doc_lengths: int32 [32, 4], P('dp'), may hold values from 1 to 128, 256 in all within a row
Outputs:
- input_grad: bfloat16 [8192, 4096], P(('dp', 'tensor'))
- query_weight_grad: float32 [4096, 4096], P('dp', 'tensor')
- kv_weight_grad: float32 [4096, 1024], P('dp', 'tensor')
Inputs may be any that keep to these rules, and one draw needn't show every extreme that they name: `doc_lengths`: each row sums to 256.
All inputs are finite; a program needn't handle non-finite values.
Results may differ from a plain program's by a relative error of at most 0.025.
Values may be sent and summed in bfloat16 or wider, within the bound.
A program may use at most 64 MiB of HBM per device.

v0:
```python
import math
import jax
import jax.numpy as jnp
from jax import lax
from jax.sharding import PartitionSpec as P

KVH = 4
HD = 128
epsilon = 1e-05


def partner_2(value, axis, bit):
    mask = 2**bit
    pairs = [(source, source ^ mask) for source in range(lax.axis_size(axis))]
    return lax.ppermute(value, axis, pairs)


def document_mask(lengths, length_total):
    ends = jnp.cumsum(lengths)
    positions = jnp.arange(length_total, dtype=jnp.int32)
    labels = jnp.sum((ends[None, :] <= positions[:, None]).astype(jnp.int32), axis=1)
    return (labels[:, None] == labels[None, :]) & (positions[None, :] <= positions[:, None])


def local(tokens, norm_gain, query_weight, kv_weight, out_weight, grad_out, doc_lengths):
    tensor_size = lax.axis_size("tensor")
    data_size = lax.axis_size("dp")
    tensor_index = lax.axis_index("tensor")
    sharers = tensor_size // KVH
    levels = sharers.bit_length() - 1
    contract_last = (((1,), (1,)), ((), ()))
    values32 = tokens.astype(jnp.float32)
    root_mean = jnp.sqrt(jnp.mean(values32 * values32, axis=-1) + epsilon)
    unit = values32 / root_mean[:, None]
    gain32 = norm_gain.astype(jnp.float32)
    normed_local = (unit * gain32).astype(jnp.bfloat16)
    normed = lax.all_gather(normed_local, "tensor", axis=0, tiled=True)
    seq_length = normed.shape[0]
    query_full = lax.all_gather(query_weight, "dp", axis=0, tiled=True)
    queries = jnp.dot(normed, query_full, preferred_element_type=jnp.float32).astype(jnp.bfloat16)
    kv_local = lax.all_gather(kv_weight, "dp", axis=0, tiled=True)
    head_weight = kv_local
    for bit_index in range(levels):
        partner = partner_2(head_weight, "tensor", bit_index)
        joined_upper_half = tensor_index >> bit_index & 1 == 1
        head_weight = jnp.concatenate(
            [
                jnp.where(joined_upper_half, partner, head_weight),
                jnp.where(joined_upper_half, head_weight, partner),
            ],
            axis=1,
        )
    keyvals = jnp.dot(normed, head_weight, preferred_element_type=jnp.float32).astype(jnp.bfloat16)
    key_rows = keyvals[:, :HD]
    value_rows = keyvals[:, HD:]
    grad_full = lax.all_gather(grad_out, "tensor", axis=0, tiled=True)
    out_grad = lax.dot_general(
        grad_full,
        lax.all_gather(out_weight, "dp", axis=1, tiled=True),
        contract_last,
        preferred_element_type=jnp.float32,
    ).astype(jnp.bfloat16)
    local_heads = queries.shape[1] // HD
    query_heads = queries.reshape(seq_length, local_heads, HD)
    out_heads = out_grad.reshape(seq_length, local_heads, HD)
    allowed = document_mask(doc_lengths[0], seq_length)
    scores = jnp.einsum(
        "qhd,td->hqt", query_heads, key_rows, preferred_element_type=jnp.float32
    ) / math.sqrt(HD)
    scores = jnp.where(allowed[None, :, :], scores, -1e30)
    peak = jnp.max(scores, axis=-1, keepdims=True)
    expo = jnp.exp(scores - peak)
    probs = expo / jnp.sum(expo, axis=-1, keepdims=True)
    probs_low = probs.astype(jnp.bfloat16)
    prob_grad = jnp.einsum("qhd,td->hqt", out_heads, value_rows, preferred_element_type=jnp.float32)
    inner = jnp.sum(probs * prob_grad, axis=-1, keepdims=True)
    score_grad = (probs * (prob_grad - inner) / math.sqrt(HD)).astype(jnp.bfloat16)
    query_grad = jnp.einsum("hqt,td->qhd", score_grad, key_rows, preferred_element_type=jnp.float32)
    query_grad = query_grad.astype(jnp.bfloat16).reshape(seq_length, local_heads * HD)
    key_part = jnp.einsum(
        "hqt,qhd->td", score_grad, query_heads, preferred_element_type=jnp.float32
    )
    value_part = jnp.einsum("hqt,qhd->td", probs_low, out_heads, preferred_element_type=jnp.float32)
    kv_partial = jnp.concatenate([key_part, value_part], axis=1)
    for bit_index in reversed(range(levels)):
        half_cols = kv_partial.shape[1] // 2
        upper_half = tensor_index >> bit_index & 1 == 1
        lower_cols = kv_partial[:, :half_cols]
        higher_cols = kv_partial[:, half_cols:]
        kept = jnp.where(upper_half, higher_cols, lower_cols)
        handed = jnp.where(upper_half, lower_cols, higher_cols)
        kv_partial = kept + partner_2(handed.astype(jnp.bfloat16), "tensor", bit_index).astype(
            handed.dtype
        )
    kv_grad = kv_partial.astype(jnp.bfloat16)
    from_query = lax.dot_general(
        query_grad, query_full, contract_last, preferred_element_type=jnp.float32
    )
    from_kv = lax.dot_general(kv_grad, kv_local, contract_last, preferred_element_type=jnp.float32)
    normed_grad = lax.psum_scatter(
        (from_query + from_kv).astype(jnp.bfloat16), "tensor", scatter_dimension=0, tiled=True
    ).astype(jnp.float32)
    scaled = normed_grad * gain32
    correction = unit * jnp.mean(scaled * unit, axis=-1, keepdims=True)
    input_grad = (grad_out.astype(jnp.float32) + (scaled - correction) / root_mean[:, None]).astype(
        jnp.bfloat16
    )
    combined = jnp.concatenate([query_grad, kv_grad], axis=1)
    weight_grads = (
        lax.psum_scatter(
            lax.dot_general(
                normed, combined, (((0,), (0,)), ((), ())), preferred_element_type=jnp.float32
            ).astype(jnp.bfloat16),
            "dp",
            scatter_dimension=0,
            tiled=True,
        ).astype(jnp.float32)
        / data_size
    )
    query_width = query_weight.shape[1]
    return (input_grad, weight_grads[:, :query_width], weight_grads[:, query_width:])


def solution(mesh):
    placed = (
        P(("dp", "tensor"), None),
        P(),
        P("dp", "tensor"),
        P("dp", "tensor"),
        P("tensor", "dp"),
        P(("dp", "tensor"), None),
        P("dp", None),
    )
    return jax.shard_map(
        local,
        mesh=mesh,
        in_specs=placed,
        out_specs=(P(("dp", "tensor"), None), P("dp", "tensor"), P("dp", "tensor")),
        check_vma=False,
    )
```

profile of v0, /device:TPU:4, one launch (start us, length us, event | category | flops | bytes accessed | tf_op | source)
XLA Modules:
  0.0 718.5 jit_solution(1927866429500999006)
XLA Ops:
  9.0 1.7 multiply_convert_fusion
  12.2 36.2 %all_gather.16 = bf16[4096,64]{0,1:T(8,128)(2,1)S(1)} all-gather(bf16[128,64]{0,1:T(8,128)(2,1)} %param.10), channel_id=1, replica_groups=mesh['dp'=32,'tensor'=16] {'dp'}, dimensions={0}, use_global_device_ids=true | all-gather | bytes 540672 | tf_op jit(solution)/shard_map/all_gather | solution.py:41
  48.4 4.2 collective-permute-start
  52.7 12.9 %collective-permute-done = bf16[4096,64]{0,1:T(8,128)(2,1)S(1)} collective-permute-done((bf16[4096,64]{0,1:T(8,128)(2,1)S(1)}, bf16[4096,64]{0,1:T(8,128)(2,1)S(1)}, u32[]{:S(2)}, u32[]{:S(2)}) %collective-permute-start) | collective-permute-done | bytes 524320 | tf_op jit(solution)/shard_map/ppermute | solution.py:15
  66.8 5.8 collective-permute-start.1
  73.1 55.3 %collective-permute-done.1 = bf16[4096,128]{0,1:T(8,128)(2,1)S(1)} collective-permute-done((bf16[4096,128]{0,1:T(8,128)(2,1)}, bf16[4096,128]{0,1:T(8,128)(2,1)S(1)}, u32[]{:S(2)}, u32[]{:S(2)}) %collective-permute-start.1) | collective-permute-done | bytes 1048608 | tf_op jit(solution)/shard_map/ppermute | solution.py:15
  128.4 1.8 broadcast_select_fusion.1
  130.2 2.9 fusion.15
  133.1 82.9 %all-gather.9.cloned.1.call-done = bf16[256,4096]{1,0:T(8,128)(2,1)} async-done(((bf16[16,4096]{1,0:T(8,128)(2,1)}), bf16[256,4096]{1,0:T(8,128)(2,1)}) %all-gather.9.cloned.1.call-update) | async-done | bytes 2097168 | tf_op jit(solution)/shard_map/all_gather | solution.py:56
  216.0 69.3 %all-gather.11.cloned.1.call-done = bf16[256,4096]{1,0:T(8,128)(2,1)} async-done(((bf16[256,128]{1,0:T(8,128)(2,1)}), bf16[256,4096]{1,0:T(8,128)(2,1)}) %all-gather.11.cloned.1.call-update) | async-done | bytes 2097168 | tf_op jit(solution)/shard_map/all_gather | solution.py:59
  285.4 3.0 convolution_convert_fusion.2
  288.6 64.3 %all-gather.7.cloned.1.call-done = bf16[4096,256]{1,0:T(8,128)(2,1)} async-done(((bf16[128,256]{1,0:T(8,128)(2,1)}), bf16[4096,256]{1,0:T(8,128)(2,1)}) %all-gather.7.cloned.1.call-update) | async-done | bytes 2097168 | tf_op jit(solution)/shard_map/all_gather | solution.py:39
  352.9 2.5 convolution_convert_fusion.3
  358.4 4.8 collective-permute-start.2
  363.1 1.5 convolution_convert_fusion.1
  364.6 2.7 collective-permute-done.2
  368.2 2.6 collective-permute-start.3
  371.6 2.4 collective-permute-done.3
  374.0 2.1 fusion.2
  376.2 2.4 convolution_convert_fusion
  378.6 2.8 copy.38
  381.4 204.1 %reduce-scatter.5.cloned.1.call-done = bf16[16,4096]{1,0:T(8,128)(2,1)} async-done(((bf16[256,4096]{1,0:T(8,128)(2,1)}), bf16[16,4096]{1,0:T(8,128)(2,1)}) %reduce-scatter.5.cloned.1.call-update) | async-done | bytes 131088 | tf_op jit(solution)/shard_map/reduce_scatter | solution.py:100
  586.7 1.7 add_convert_fusion
  588.4 120.9 %reduce-scatter.7.cloned.1.call-done = bf16[128,320]{1,0:T(8,128)(2,1)} async-done(((bf16[4096,320]{1,0:T(8,128)(2,1)}), bf16[128,320]{1,0:T(8,128)(2,1)}) %reduce-scatter.7.cloned.1.call-update) | async-done | bytes 81936
  (56 shorter events, 13.3 us)
Async XLA Ops:
  7.2 123.0 %all-gather.5.cloned.1.call-start = ((), (), s32[]{:S(2)}) async-start(), calls=%async_computation.2 | async-start | bytes 2228224 | tf_op jit(solution)/shard_map/all_gather | solution.py:37
  8.3 0.7 copy-start.5
  10.7 205.4 %all-gather.9.cloned.1.call-start = ((), (), s32[]{:S(2)}) async-start(), calls=%async_computation.4 | async-start | bytes 2228224 | tf_op jit(solution)/shard_map/all_gather | solution.py:56
  11.4 274.0 %all-gather.11.cloned.1.call-start = ((), (), s32[]{:S(2)}) async-start(), calls=%async_computation.5 | async-start | bytes 2162688 | tf_op jit(solution)/shard_map/all_gather | solution.py:59
  12.2 340.8 %all-gather.7.cloned.1.call-start = ((), (), s32[]{:S(2)}) async-start(), calls=%async_computation.3 | async-start | bytes 2162688 | tf_op jit(solution)/shard_map/all_gather | solution.py:39
  48.4 17.2 %collective-permute-start = (bf16[4096,64]{0,1:T(8,128)(2,1)S(1)}, bf16[4096,64]{0,1:T(8,128)(2,1)S(1)}, u32[]{:S(2)}, u32[]{:S(2)}) collective-permute-start(bf16[4096,64]{0,1:T(8,128)(2,1)S(1)} %all_gather.16), channel_id=1, source_target_pairs={{0,1},{1,0},{2,3},{3,2},{4,5},{5,4},{6,7},{7,6},{8,9},{9,8},{10,11... | collective-permute-start | bytes 1572872 | tf_op jit(solution)/shard_map/ppermute | solution.py:15
  52.6 532.9 %reduce-scatter.5.cloned.1.call-start = ((), (), s32[]{:S(2)}) async-start(), calls=%async_computation.6 | async-start | bytes 2228224 | tf_op jit(solution)/shard_map/reduce_scatter | solution.py:100
  52.7 20.0 %copy-start.7 = (s32[1,4]{1,0:T(1,128)S(1)}, s32[1,4]{1,0:T(1,128)}, u32[]{:S(2)}) copy-start(s32[1,4]{1,0:T(1,128)} %param.13) | copy-start | bytes 52
  66.8 61.5 %collective-permute-start.1 = (bf16[4096,128]{0,1:T(8,128)(2,1)}, bf16[4096,128]{0,1:T(8,128)(2,1)S(1)}, u32[]{:S(2)}, u32[]{:S(2)}) collective-permute-start(bf16[4096,128]{0,1:T(8,128)(2,1)} %pad_maximum_fusion), channel_id=1, source_target_pairs={{0,2},{1,3},{2,0},{3,1},{4,6},{5,7},{6,4},{7,5},{8,10},{9,11},{10,... | collective-permute-start | bytes 3145736 | tf_op jit(solution)/shard_map/ppermute | solution.py:15
  133.1 155.2 %copy-start.4 = (bf16[256,256]{1,0:T(8,128)(2,1)}, bf16[256,256]{1,0:T(8,128)(2,1)S(1)}, u32[]{:S(2)}) copy-start(bf16[256,256]{1,0:T(8,128)(2,1)S(1)} %fusion.15) | copy-start | bytes 393220
  133.1 219.8 %copy-start.1 = (bf16[256,4096]{1,0:T(8,128)(2,1)S(1)}, bf16[256,4096]{1,0:T(8,128)(2,1)}, u32[]{:S(2)}) copy-start(bf16[256,4096]{1,0:T(8,128)(2,1)} %all-gather.5.cloned.1.call-done) | copy-start | bytes 6291460
  356.6 0.8 copy-start.8
  356.6 0.8 copy-start.9
  358.4 12.5 %copy-start = (bf16[4096,256]{1,0:T(8,128)(2,1)S(1)}, bf16[4096,256]{1,0:T(8,128)(2,1)}, u32[]{:S(2)}) copy-start(bf16[4096,256]{1,0:T(8,128)(2,1)} %all-gather.7.cloned.1.call-done) | copy-start | bytes 6291460
  358.4 9.0 %collective-permute-start.2 = (bf16[256,128]{0,1:T(8,128)(2,1)}, bf16[256,128]{0,1:T(8,128)(2,1)}, u32[]{:S(2)}, u32[]{:S(2)}) collective-permute-start(bf16[256,128]{0,1:T(8,128)(2,1)} %get-tuple-element.18), channel_id=1, source_target_pairs={{0,2},{1,3},{2,0},{3,1},{4,6},{5,7},{6,4},{7,5},{8,10},{9,11},{10,... | collective-permute-start | bytes 196616 | tf_op jit(solution)/shard_map/ppermute | solution.py:15
  368.2 5.8 collective-permute-start.3
  376.1 333.2 %reduce-scatter.7.cloned.1.call-start = ((), (), s32[]{:S(2)}) async-start(), calls=%async_computation.7 | async-start | bytes 3244032
  381.4 204.1 %copy-start.2 = (bf16[16,4096]{1,0:T(8,128)(2,1)S(1)}, bf16[16,4096]{1,0:T(8,128)(2,1)}, u32[]{:S(2)}) copy-start(bf16[16,4096]{1,0:T(8,128)(2,1)} %param.7) | copy-start | bytes 393220
  381.4 204.1 %copy-start.6 = (f32[16]{0:T(128)S(1)}, f32[16]{0:T(128)}, u32[]{:S(2)}) copy-start(f32[16]{0:T(128)} %copy-done.5) | copy-start | bytes 196
  381.4 205.3 %copy-start.3 = (bf16[16,4096]{1,0:T(8,128)(2,1)S(1)}, bf16[16,4096]{1,0:T(8,128)(2,1)}, u32[]{:S(2)}) copy-start(bf16[16,4096]{1,0:T(8,128)(2,1)} %param.12) | copy-start | bytes 393220
Sparse Core Ops, SparseCore 0:
  11.7 109.4 all-gather.4
  124.4 91.6 all-gather.8
  218.1 67.2 all-gather.10
  287.4 65.4 all-gather.6
  376.2 209.2 reduce-scatter.4
  588.2 121.0 reduce-scatter.6
where the time goes:
time: 719 us
  waiting for transfers between devices  616 us (86%)
  blocking collectives  36.2 us (5%)
  matrix products  17.7 us (2%)
  starting transfers between devices  17.6 us (2%)
  between operations  14.3 us (2%)
  other arithmetic  10.6 us (1%)
    reduce_scatter x1, waiting for transfers between devices, local(): lax.psum_scatter((from_query + from_kv).astype(jnp.bfloat16), 'tensor', s...  204 us
    unnamed x7, waiting for transfers between devices  122 us
    all_gather x1, waiting for transfers between devices, local(): grad_full = lax.all_gather(grad_out, 'tensor', axis=0, tiled=True)  82.9 us
    ppermute x4, waiting for transfers between devices, partner_2(): return lax.ppermute(value, axis, pairs)  73.3 us
    all_gather x1, waiting for transfers between devices, local(): lax.all_gather(out_weight, 'dp', axis=1, tiled=True)  69.3 us
    all_gather x1, waiting for transfers between devices, local(): query_full = lax.all_gather(query_weight, 'dp', axis=0, tiled=True)  64.3 us
    all_gather x1, blocking collectives, local(): kv_local = lax.all_gather(kv_weight, 'dp', axis=0, tiled=True)  36.2 us
    ppermute x4, starting transfers between devices, partner_2(): return lax.ppermute(value, axis, pairs)  17.4 us
  transfers between devices with their start and end apart: 10, of which 9 were waited for; matrix products, arithmetic and copies ran while one was open for 3% of the time, Pallas kernels for 0%

commit v1 on v0

--- a/solution.py
+++ b/solution.py
@@ -56,7 +56,9 @@
     grad_full = lax.all_gather(grad_out, "tensor", axis=0, tiled=True)
     out_grad = lax.dot_general(
         grad_full,
-        lax.all_gather(out_weight, "dp", axis=1, tiled=True),
+        jnp.concatenate(
+            lax.all_to_all(jnp.stack([out_weight] * lax.axis_size("dp")), "dp", 0, 0), axis=1
+        ),
         contract_last,
         preferred_element_type=jnp.float32,
     ).astype(jnp.bfloat16)

time: 719 us -> 648 us (0.901)
  waiting for transfers between devices: 616 us -> 539 us
    all_gather x1 -> x0, waiting for transfers between devices: 69.3 us -> none  [local(): lax.all_gather(out_weight, 'dp', axis=1, tiled=True)]
    ppermute x4, waiting for transfers between devices: 73.3 us -> 66 us  [partner_2(): return lax.ppermute(value, axis, pairs)]
    unnamed x7 -> x6, waiting for transfers between devices: 122 us -> 122 us
  transfers between devices with their start and end apart: 10 -> 10, of which waited for: 9 -> 8; matrix products, arithmetic and copies ran while one was open for 3% -> 4% of each run, Pallas kernels for 0% -> 0%
where the time goes in v1:
time: 648 us
  waiting for transfers between devices  539 us (83%)
  blocking collectives  36.2 us (6%)
  starting transfers between devices  21.6 us (3%)
  matrix products  16.4 us (3%)
  between operations  14 us (2%)
  other arithmetic  12 us (2%)
  local copies, waits for them, and re-layouts  8.27 us (1%)
    reduce_scatter x1, waiting for transfers between devices, local(): lax.psum_scatter((from_query + from_kv).astype(jnp.bfloat16), 'tensor', s...  204 us
    unnamed x6, waiting for transfers between devices  122 us
    all_gather x1, waiting for transfers between devices, local(): grad_full = lax.all_gather(grad_out, 'tensor', axis=0, tiled=True)  81.9 us
    ppermute x4, waiting for transfers between devices, partner_2(): return lax.ppermute(value, axis, pairs)  66 us
    all_gather x1, waiting for transfers between devices, local(): query_full = lax.all_gather(query_weight, 'dp', axis=0, tiled=True)  65.2 us
    all_gather x1, blocking collectives, local(): kv_local = lax.all_gather(kv_weight, 'dp', axis=0, tiled=True)  36.2 us
    ppermute x4, starting transfers between devices, partner_2(): return lax.ppermute(value, axis, pairs)  17.3 us
  transfers between devices with their start and end apart: 10, of which 8 were waited for; matrix products, arithmetic and copies ran while one was open for 4% of the time, Pallas kernels for 0%

profile of v1, /device:TPU:4, one launch (start us, length us, event | category | flops | bytes accessed | tf_op | source)
XLA Modules:
  0.0 647.5 jit_solution(18058437337988467007)
XLA Ops:
  9.0 1.7 multiply_convert_fusion
  11.4 36.2 %all_gather.13 = bf16[4096,64]{0,1:T(8,128)(2,1)S(1)} all-gather(bf16[128,64]{0,1:T(8,128)(2,1)} %param.10), channel_id=1, replica_groups=mesh['dp'=32,'tensor'=16] {'dp'}, dimensions={0}, use_global_device_ids=true | all-gather | bytes 540672 | tf_op jit(solution)/shard_map/all_gather | solution.py:41
  47.6 4.3 collective-permute-start
  52.9 1.6 stack.2
  54.5 4.0 all-to-all-start
  59.3 5.9 collective-permute-done
  67.5 5.7 collective-permute-start.1
  73.5 55.4 %collective-permute-done.1 = bf16[4096,128]{0,1:T(8,128)(2,1)} collective-permute-done((bf16[4096,128]{0,1:T(8,128)(2,1)}, bf16[4096,128]{0,1:T(8,128)(2,1)}, u32[]{:S(2)}, u32[]{:S(2)}) %collective-permute-start.1) | collective-permute-done | bytes 1048608 | tf_op jit(solution)/shard_map/ppermute | solution.py:15
  128.9 3.0 broadcast_select_fusion.1
  131.9 2.9 fusion.15
  134.8 81.9 %all-gather.8.cloned.1.call-done = bf16[256,4096]{1,0:T(8,128)(2,1)} async-done(((bf16[16,4096]{1,0:T(8,128)(2,1)}), bf16[256,4096]{1,0:T(8,128)(2,1)}) %all-gather.8.cloned.1.call-update) | async-done | bytes 2097168 | tf_op jit(solution)/shard_map/all_gather | solution.py:56
  216.7 2.5 convolution_convert_fusion.2
  219.5 65.2 %all-gather.6.cloned.1.call-done = bf16[4096,256]{1,0:T(8,128)(2,1)} async-done(((bf16[128,256]{1,0:T(8,128)(2,1)}), bf16[4096,256]{1,0:T(8,128)(2,1)}) %all-gather.6.cloned.1.call-update) | async-done | bytes 2097168 | tf_op jit(solution)/shard_map/all_gather | solution.py:39
  284.6 3.1 convolution_convert_fusion.3
  289.2 4.8 collective-permute-start.2
  295.5 2.4 collective-permute-done.2
  297.9 2.6 collective-permute-start.3
  301.3 2.4 collective-permute-done.3
  303.7 2.1 fusion.2
  305.9 2.4 convolution_convert_fusion
  308.4 2.8 copy.48
  311.2 204.0 %reduce-scatter.5.cloned.1.call-done = bf16[16,4096]{1,0:T(8,128)(2,1)} async-done(((bf16[256,4096]{1,0:T(8,128)(2,1)}), bf16[16,4096]{1,0:T(8,128)(2,1)}) %reduce-scatter.5.cloned.1.call-update) | async-done | bytes 131088 | tf_op jit(solution)/shard_map/reduce_scatter | solution.py:102
  516.3 1.7 add_convert_fusion
  518.0 120.5 %reduce-scatter.7.cloned.1.call-done = bf16[128,320]{1,0:T(8,128)(2,1)} async-done(((bf16[4096,320]{1,0:T(8,128)(2,1)}), bf16[128,320]{1,0:T(8,128)(2,1)}) %reduce-scatter.7.cloned.1.call-update) | async-done | bytes 81936
  (51 shorter events, 14.5 us)
Async XLA Ops:
  7.2 124.7 %all-gather.4.cloned.1.call-start = ((), (), s32[]{:S(2)}) async-start(), calls=%async_computation.3 | async-start | bytes 2228224 | tf_op jit(solution)/shard_map/all_gather | solution.py:37
  10.7 206.1 %all-gather.8.cloned.1.call-start = ((), (), s32[]{:S(2)}) async-start(), calls=%async_computation.5 | async-start | bytes 2228224 | tf_op jit(solution)/shard_map/all_gather | solution.py:56
  47.6 6.8 %copy-start.1 = (bf16[4096,64]{0,1:T(8,128)(2,1)}, bf16[4096,64]{0,1:T(8,128)(2,1)S(1)}, u32[]{:S(2)}) copy-start(bf16[4096,64]{0,1:T(8,128)(2,1)S(1)} %all_gather.13) | copy-start | bytes 1572868
  47.6 17.5 %collective-permute-start = (bf16[4096,64]{0,1:T(8,128)(2,1)S(1)}, bf16[4096,64]{0,1:T(8,128)(2,1)}, u32[]{:S(2)}, u32[]{:S(2)}) collective-permute-start(bf16[4096,64]{0,1:T(8,128)(2,1)S(1)} %all_gather.13), channel_id=1, source_target_pairs={{0,1},{1,0},{2,3},{3,2},{4,5},{5,4},{6,7},{7,6},{8,9},{9,8},{10,11... | collective-permute-start | bytes 1572872 | tf_op jit(solution)/shard_map/ppermute | solution.py:15
  54.5 162.3 %all-to-all-start = ((bf16[32,256,128]{1,2,0:T(8,128)(2,1)}), bf16[32,256,128]{1,2,0:T(8,128)(2,1)S(1)}, u32[]{:S(2)}, u32[]{:S(2)}) async-start(bf16[32,256,128]{1,2,0:T(8,128)(2,1)} %stack.2), calls=%async_computation | async-start | bytes 4194304 | tf_op jit(solution)/shard_map/all_to_all | solution.py:60
  58.5 226.2 %all-gather.6.cloned.1.call-start = ((), (), s32[]{:S(2)}) async-start(), calls=%async_computation.4 | async-start | bytes 2162688 | tf_op jit(solution)/shard_map/all_gather | solution.py:39
  59.2 456.0 %reduce-scatter.5.cloned.1.call-start = ((), (), s32[]{:S(2)}) async-start(), calls=%async_computation.6 | async-start | bytes 2228224 | tf_op jit(solution)/shard_map/reduce_scatter | solution.py:102
  59.3 13.9 %copy-start.5 = (s32[1,4]{1,0:T(1,128)S(1)}, s32[1,4]{1,0:T(1,128)}, u32[]{:S(2)}) copy-start(s32[1,4]{1,0:T(1,128)} %param.13) | copy-start | bytes 52
  67.5 61.4 %collective-permute-start.1 = (bf16[4096,128]{0,1:T(8,128)(2,1)}, bf16[4096,128]{0,1:T(8,128)(2,1)}, u32[]{:S(2)}, u32[]{:S(2)}) collective-permute-start(bf16[4096,128]{0,1:T(8,128)(2,1)} %pad_maximum_fusion), channel_id=1, source_target_pairs={{0,2},{1,3},{2,0},{3,1},{4,6},{5,7},{6,4},{7,5},{8,10},{9,11},{10,... | collective-permute-start | bytes 3145736 | tf_op jit(solution)/shard_map/ppermute | solution.py:15
  288.1 0.8 copy-start.6
  289.2 11.3 %copy-start = (bf16[4096,256]{1,0:T(8,128)(2,1)S(1)}, bf16[4096,256]{1,0:T(8,128)(2,1)}, u32[]{:S(2)}) copy-start(bf16[4096,256]{1,0:T(8,128)(2,1)} %all-gather.6.cloned.1.call-done) | copy-start | bytes 6291460
  289.2 8.7 %collective-permute-start.2 = (bf16[256,128]{0,1:T(8,128)(2,1)S(1)}, bf16[256,128]{0,1:T(8,128)(2,1)S(1)}, u32[]{:S(2)}, u32[]{:S(2)}) collective-permute-start(bf16[256,128]{0,1:T(8,128)(2,1)S(1)} %get-tuple-element.21), channel_id=1, source_target_pairs={{0,2},{1,3},{2,0},{3,1},{4,6},{5,7},{6,4},{7,5},{8,10},{9,11},{10,... | collective-permute-start | bytes 196616 | tf_op jit(solution)/shard_map/ppermute | solution.py:15
  297.9 5.8 collective-permute-start.3
  300.6 3.2 copy-start.2
  305.9 332.7 %reduce-scatter.7.cloned.1.call-start = ((), (), s32[]{:S(2)}) async-start(), calls=%async_computation.7 | async-start | bytes 3244032
  311.1 204.1 %copy-start.3 = (bf16[16,4096]{1,0:T(8,128)(2,1)S(1)}, bf16[16,4096]{1,0:T(8,128)(2,1)}, u32[]{:S(2)}) copy-start(bf16[16,4096]{1,0:T(8,128)(2,1)} %param.7) | copy-start | bytes 393220
  311.1 205.2 %copy-start.4 = (bf16[16,4096]{1,0:T(8,128)(2,1)S(1)}, bf16[16,4096]{1,0:T(8,128)(2,1)}, u32[]{:S(2)}) copy-start(bf16[16,4096]{1,0:T(8,128)(2,1)} %param.12) | copy-start | bytes 393220
Sparse Core Ops, SparseCore 0:
  11.7 109.5 all-gather.3
  124.5 92.1 all-gather.7
  218.9 65.6 all-gather.5
  306.0 209.1 reduce-scatter.4
  517.9 120.6 reduce-scatter.6
